TPU v7x, 32 devices: a whole 2x2x4 slice. The times are simulated.
32 devices in a mesh: groups: 2 (over y), space: 4 (over z), tm: 2 (over x), chan: 2 (over core).
Axes of the slice: x: 2, y: 2, z: 4, core: 2. Of those that a mesh axis runs over, the one named last changes fastest.
Arguments:
- hidden_states: bfloat16 [8, 4, 64, 512], P(('groups', 'tm'), 'space', None, 'chan'), parts along dimension 0, may hold values from -25 to 25
- first_gain: float32 [512], P('chan'), may hold values from 0.1 to 1.9
- second_gain: float32 [512], P('chan'), may hold values from 0.1 to 1.9
- query_weight: bfloat16 [512, 512], replicated, may hold values from -0.4861359 to 0.4861359
- key_weight: bfloat16 [512, 512], replicated, may hold values from -0.4861359 to 0.4861359
- value_weight: bfloat16 [512, 512], replicated, may hold values from -0.25 to 0.25
- out_weight: bfloat16 [512, 512], replicated, may hold values from -0.25 to 0.25
- conv_kernel: bfloat16 [3, 3, 3, 512, 512], P(None, None, None, 'tm', 'chan'), may hold values from -0.0546875 to 0.0546875
Outputs:
- attended: bfloat16 [8, 4, 64, 512], P(('groups', 'tm'), 'space', None, 'chan'), parts along dimension 0
- convolved: bfloat16 [8, 4, 64, 512], P(('groups', 'tm'), 'space', None, 'chan'), parts along dimension 0
There are 2 independent parts, one for each index of `groups`. A program takes and returns all parts, laid end to end along the dimension named above; an argument that names none is the same for every part. Nothing has to cross between parts.
All inputs are finite; a program needn't handle non-finite values.
Results may differ from a plain program's by a relative error of at most 0.012.
The roundings to bfloat16 on the way count: a program that leaves them out, or rounds other values in their place, can miss the bound.
Values may be sent and summed in bfloat16 or wider, within the bound.
A program may use at most 64 MiB of HBM per device.

v0:
```python
import jax
import jax.numpy as jnp
from jax import lax
from jax.sharding import PartitionSpec as P

D = 512
NGROUP = 32


EPSILON = 1e-06


def shifted_2(x, axis, by):
    peers = lax.axis_size(axis)
    pairs = [(i, i + by) for i in range(peers) if 0 <= i + by < peers]
    return lax.ppermute(x, axis, pairs)


def padded_2(cells, sides, width):
    for axis, dim in sides:
        count = lax.axis_size(axis)
        ends = count - 1
        head = lax.slice_in_dim(cells, 0, width, axis=dim)
        tail = lax.slice_in_dim(cells, cells.shape[dim] - width, cells.shape[dim], axis=dim)
        cells = jnp.concatenate(
            [
                lax.ppermute(tail, axis, [(i, (i + 1) % count) for i in range(ends)]),
                cells,
                lax.ppermute(head, axis, [((i + 1) % count, i) for i in range(ends)]),
            ],
            axis=dim,
        )
    return cells


def normalize(source, gain_vector):
    channels = source.shape[3]
    group_width = D // NGROUP
    grouped = source.reshape(-1, channels // group_width, group_width)
    population = grouped.shape[0] * group_width * lax.axis_size("space") * lax.axis_size("tm")
    group_sums, group_squares = lax.psum(
        (jnp.sum(grouped, axis=(0, 2)), jnp.sum(grouped * grouped, axis=(0, 2))), ("space", "tm")
    )
    centre = group_sums / population
    spread = jnp.maximum(group_squares / population - centre * centre, 0.0)
    shifted = grouped - centre[None, :, None]
    scaled = shifted * lax.rsqrt(spread + EPSILON)[None, :, None]
    return scaled.reshape(source.shape) * gain_vector


def attend(normed, query_weight, key_weight, value_weight, out_weight):
    frame_count, row_count, col_count, channels = normed.shape
    token_count = frame_count * row_count * col_count
    tokens = normed.reshape(token_count, channels)
    halves = lax.all_to_all(tokens, "chan", split_axis=0, concat_axis=1, tiled=True)
    half_rows = halves.shape[0]
    queries = jnp.dot(halves, query_weight, preferred_element_type=jnp.float32).astype(jnp.bfloat16)
    keyed = jnp.dot(halves, key_weight, preferred_element_type=jnp.float32).astype(jnp.bfloat16)
    valued = jnp.dot(halves, value_weight, preferred_element_type=jnp.float32).astype(jnp.bfloat16)
    score_scale = D ** (-0.5)
    running_max = jnp.full((half_rows,), -1e30, jnp.float32)
    key_piece = lax.all_gather(keyed, "space", axis=0, tiled=True)
    value_piece = lax.all_gather(valued, "space", axis=0, tiled=True)
    scores = jnp.dot(queries, key_piece.T, preferred_element_type=jnp.float32) * score_scale
    newest_max = jnp.maximum(running_max, jnp.max(scores, axis=1))
    weights = jnp.exp(scores - newest_max[:, None])
    running_sum = jnp.sum(weights, axis=1)
    accumulated = jnp.dot(
        weights.astype(jnp.bfloat16), value_piece, preferred_element_type=jnp.float32
    )
    mixed = (accumulated / running_sum[:, None]).astype(jnp.bfloat16)
    projected = jnp.dot(mixed, out_weight, preferred_element_type=jnp.float32).astype(jnp.bfloat16)
    returned = lax.all_to_all(projected, "chan", split_axis=1, concat_axis=0, tiled=True)
    return returned.reshape(frame_count, row_count, col_count, channels)


def join_channels(activated):
    return lax.all_gather(activated, "chan", axis=3, tiled=True)


def extend(frames_in):
    earlier = shifted_2(frames_in, "tm", 1)
    timed = jnp.concatenate([earlier, frames_in], axis=0)
    rimmed = padded_2(timed, (("space", 1),), 1)
    return jnp.pad(rimmed, ((0, 0), (0, 0), (1, 1), (0, 0)))


def convolve(activated, conv_kernel):
    frame_count, row_count, col_count = (activated.shape[0], activated.shape[1], activated.shape[2])
    padded = extend(join_channels(activated))
    out_width = conv_kernel.shape[4]
    initial = jnp.zeros((frame_count * row_count * col_count, out_width), jnp.float32)
    running_total = initial
    piece = lax.all_gather(conv_kernel, "tm", axis=3, tiled=True)
    for time_tap in range(3):
        for row_tap in range(3):
            for col_tap in range(3):
                window = padded[
                    time_tap : time_tap + frame_count,
                    row_tap : row_tap + row_count,
                    col_tap : col_tap + col_count,
                ]
                window = window.reshape(frame_count * row_count * col_count, piece.shape[3])
                running_total = running_total + jnp.dot(
                    window, piece[time_tap, row_tap, col_tap], preferred_element_type=jnp.float32
                )
    return running_total.reshape(frame_count, row_count, col_count, out_width).astype(jnp.bfloat16)


def on_device(
    hidden_states,
    first_gain,
    second_gain,
    query_weight,
    key_weight,
    value_weight,
    out_weight,
    conv_kernel,
):
    source = hidden_states.astype(jnp.float32)
    normed = normalize(source, first_gain).astype(jnp.bfloat16)
    attended = attend(normed, query_weight, key_weight, value_weight, out_weight)
    resid = source + attended.astype(jnp.float32)
    activated = jax.nn.silu(normalize(resid, second_gain)).astype(jnp.bfloat16)
    convolved = convolve(activated, conv_kernel)
    return (attended, convolved)


def solution(mesh):
    placed = (
        P(("groups", "tm"), "space", None, "chan"),
        P("chan"),
        P("chan"),
        P(),
        P(),
        P(),
        P(),
        P(None, None, None, "tm", "chan"),
    )
    return jax.shard_map(
        on_device,
        mesh=mesh,
        in_specs=placed,
        out_specs=(
            P(("groups", "tm"), "space", None, "chan"),
            P(("groups", "tm"), "space", None, "chan"),
        ),
        check_vma=False,
    )
```

profile of v0, /device:TPU:0, one launch (start us, length us, event | category | flops | bytes accessed | tf_op | source)
XLA Modules:
  0.0 143.7 jit_solution(14035605134556565551)
XLA Ops:
  7.2 0.7 all-gather.2.cloned.1.call-update
  7.9 0.9 convert_reduce_fusion
  9.2 23.3 %all-reduce.2 = (f32[16]{0:T(128)S(1)}, f32[16]{0:T(128)S(1)}) all-reduce(f32[16]{0:T(128)S(1)} %reduce_sum.62, f32[16]{0:T(128)S(1)} %reduce_sum.59), channel_id=1, replica_groups=mesh['groups'=2,'space'=4,'tm'=2,'chan'=2] {'space','tm'}, use_global_device_ids=true, to_apply=%region_5.0 | all-reduce | flops 32 | bytes 256 | tf_op jit(solution)/shard_map/psum | solution.py:41
  32.9 0.9 fusion.26
  33.7 3.8 %all_to_all.35 = bf16[2,64,256]{2,1,0:T(8,128)(2,1)S(1)} all-to-all(bf16[2,64,256]{2,1,0:T(8,128)(2,1)S(1)} %fusion.26), channel_id=1, replica_groups=mesh['groups'=2,'space'=4,'tm'=2,'chan'=2] {'chan'}, dimensions={0} | all-to-all | bytes 131072 | tf_op jit(solution)/shard_map/all_to_all | solution.py:55
  37.5 0.2 convolution_convert_fusion.2
  37.8 14.3 %all_gather.12 = bf16[256,512]{1,0:T(8,128)(2,1)S(1)} all-gather(bf16[64,512]{1,0:T(8,128)(2,1)S(1)} %convolution_convert_fusion.2), channel_id=1, replica_groups=mesh['groups'=2,'space'=4,'tm'=2,'chan'=2] {'space'}, dimensions={0}, use_global_device_ids=true | all-gather | bytes 327680 | tf_op jit(solution)/shard_map/all_gather | solution.py:62
  52.1 1.2 convolution_convert_fusion.1
  53.3 13.9 %all_gather.13 = bf16[256,512]{1,0:T(8,128)(2,1)S(1)} all-gather(bf16[64,512]{1,0:T(8,128)(2,1)S(1)} %convolution_convert_fusion.1), channel_id=1, replica_groups=mesh['groups'=2,'space'=4,'tm'=2,'chan'=2] {'space'}, dimensions={0}, use_global_device_ids=true | all-gather | bytes 327680 | tf_op jit(solution)/shard_map/all_gather | solution.py:63
  67.2 1.5 %fusion.37 = (f32[64]{0:T(128)S(1)}, f32[64,256]{1,0:T(8,128)S(1)}) fusion(bf16[256,512]{1,0:T(8,128)(2,1)S(1)} %all_gather.12, bf16[64,512]{1,0:T(8,128)(2,1)S(1)} %bitcast.164, bf16[512,512]{1,0:T(8,128)(2,1)} %param.11), kind=kOutput, calls=%fused_computation.104 | convolution fusion | flops 50397120 | bytes 917760 | tf_op jit(solution)/shard_map/dot_general | solution.py:64
  68.9 1.4 convolution_convert_fusion
  70.3 3.8 %all_to_all.36 = bf16[64,2,256]{2,0,1:T(8,128)(2,1)S(1)} all-to-all(bf16[64,2,256]{2,0,1:T(8,128)(2,1)S(1)} %bitcast.193), channel_id=1, replica_groups=mesh['groups'=2,'space'=4,'tm'=2,'chan'=2] {'chan'}, dimensions={1} | all-to-all | bytes 131072 | tf_op jit(solution)/shard_map/all_to_all | solution.py:73
  74.6 17.4 %all-reduce.1 = (f32[16]{0:T(128)S(1)}, f32[16]{0:T(128)S(1)}) all-reduce(f32[16]{0:T(128)S(1)} %reduce_sum.85, f32[16]{0:T(128)S(1)} %reduce_sum.82), channel_id=1, replica_groups=mesh['groups'=2,'space'=4,'tm'=2,'chan'=2] {'space','tm'}, use_global_device_ids=true, to_apply=%region_13.14 | all-reduce | flops 32 | bytes 256 | tf_op jit(solution)/shard_map/psum | solution.py:41
  92.4 1.9 %all_gather.14 = bf16[2,1,64,512]{3,2,1,0:T(8,128)(2,1)S(1)} all-gather(bf16[2,1,64,256]{3,2,1,0:T(8,128)(2,1)S(1)} %multiply_convert_fusion), channel_id=1, replica_groups=mesh['groups'=2,'space'=4,'tm'=2,'chan'=2] {'chan'}, dimensions={3}, use_global_device_ids=true | all-gather | bytes 196608 | tf_op jit(solution)/shard_map/all_gather | solution.py:78
  94.3 4.1 %collective-permute-start = (bf16[2,1,64,512]{3,2,1,0:T(8,128)(2,1)S(1)}, bf16[2,1,64,512]{3,2,1,0:T(8,128)(2,1)S(1)}, u32[]{:S(2)}, u32[]{:S(2)}) collective-permute-start(bf16[2,1,64,512]{3,2,1,0:T(8,128)(2,1)S(1)} %all_gather.14), channel_id=1, source_target_pairs={{0,2},{1,3},{4,6},{5,7},{8,10},{9,11},{12,14},{13,15},{16,18},{17,... | collective-permute-start | bytes 393224 | tf_op jit(solution)/shard_map/ppermute | solution.py:16
  98.4 4.3 %collective-permute-done = bf16[2,1,64,512]{3,2,1,0:T(8,128)(2,1)S(1)} collective-permute-done((bf16[2,1,64,512]{3,2,1,0:T(8,128)(2,1)S(1)}, bf16[2,1,64,512]{3,2,1,0:T(8,128)(2,1)S(1)}, u32[]{:S(2)}, u32[]{:S(2)}) %collective-permute-start) | collective-permute-done | bytes 131104 | tf_op jit(solution)/shard_map/ppermute | solution.py:16
  102.8 3.0 %collective-permute-start.1 = (bf16[4,1,64,512]{3,2,1,0:T(8,128)(2,1)S(1)}, bf16[4,1,64,512]{3,2,1,0:T(8,128)(2,1)S(1)}, u32[]{:S(2)}, u32[]{:S(2)}) collective-permute-start(bf16[4,1,64,512]{3,2,1,0:T(8,128)(2,1)S(1)} %constant_dynamic-update-slice_fusion), channel_id=1, source_target_pairs={{0,4},{4,8},{8,12},{1,5},{5,9},{9,13},{2,6},{6,10},{10,14},{3,7},{... | collective-permute-start | bytes 786440 | tf_op jit(solution)/shard_map/ppermute | solution.py:27
  105.8 1.3 collective-permute-start.2
  107.1 3.8 %collective-permute-done.1 = bf16[4,1,64,512]{3,2,1,0:T(8,128)(2,1)S(1)} collective-permute-done((bf16[4,1,64,512]{3,2,1,0:T(8,128)(2,1)S(1)}, bf16[4,1,64,512]{3,2,1,0:T(8,128)(2,1)S(1)}, u32[]{:S(2)}, u32[]{:S(2)}) %collective-permute-start.1) | collective-permute-done | bytes 262176 | tf_op jit(solution)/shard_map/ppermute | solution.py:27
  110.9 4.1 %collective-permute-done.2 = bf16[4,1,64,512]{3,2,1,0:T(8,128)(2,1)S(1)} collective-permute-done((bf16[4,1,64,512]{3,2,1,0:T(8,128)(2,1)S(1)}, bf16[4,1,64,512]{3,2,1,0:T(8,128)(2,1)S(1)}, u32[]{:S(2)}, u32[]{:S(2)}) %collective-permute-start.2) | collective-permute-done | bytes 262176 | tf_op jit(solution)/shard_map/ppermute | solution.py:29
  115.0 0.2 fusion.13
  115.3 0.7 fusion.36
  116.0 0.8 fusion.35
  116.8 0.4 fusion.34
  117.2 1.3 fusion.20
  118.5 1.7 %fusion.19 = f32[128,256]{1,0:T(8,128)S(1)} fusion(bf16[128,512]{1,0:T(8,128)(2,1)S(1)} %bitcast.184, bf16[3,3,3,512,256]{4,3,2,1,0:T(8,128)(2,1)} %all-gather.2.cloned.1.call-done), kind=kOutput, calls=%fused_computation.69 | convolution fusion | flops 33554432 | bytes 524288 | tf_op jit(solution)/shard_map/dot_general | solution.py:104
  120.2 1.1 fusion.18
  121.4 1.1 fusion.17
  122.5 1.1 fusion.16
  123.7 1.2 fusion.15
  124.8 1.1 fusion.14
  126.0 1.1 convolution_add_fusion.19
  127.1 1.1 convolution_add_fusion.18
  128.3 1.1 convolution_add_fusion.17
  129.4 1.1 fusion.6
  130.6 1.1 convolution_add_fusion.15
  131.7 1.1 fusion.5
  133.0 0.2 fusion.4
  133.2 0.2 convolution_add_fusion.11
  133.4 0.2 convolution_add_fusion.10
  133.6 0.2 convolution_add_fusion.9
  133.8 0.2 convolution_add_fusion.8
  134.0 0.2 fusion.3
  134.2 0.2 convolution_add_fusion.6
  134.6 0.2 convolution_add_fusion.4
  135.0 0.2 convolution_add_fusion.2
  135.4 0.8 fusion.8
  136.3 0.6 copy.24
  (49 shorter events, 2.6 us)
Async XLA Ops:
  7.2 30.4 %copy-start = (bf16[512,512]{1,0:T(8,128)(2,1)S(1)}, bf16[512,512]{1,0:T(8,128)(2,1)}, u32[]{:S(2)}) copy-start(bf16[512,512]{1,0:T(8,128)(2,1)} %param.12) | copy-start | bytes 1572868
  7.2 67.0 %copy-start.2 = (bf16[2,1,64,256]{3,2,1,0:T(8,128)(2,1)S(1)}, bf16[2,1,64,256]{3,2,1,0:T(8,128)(2,1)}, u32[]{:S(2)}) copy-start(bf16[2,1,64,256]{3,2,1,0:T(8,128)(2,1)} %param.8) | copy-start | bytes 196612
  7.2 85.1 %copy-start.7 = (f32[256]{0:T(256)S(1)}, f32[256]{0:T(256)}, u32[]{:S(2)}) copy-start(f32[256]{0:T(256)} %param.10) | copy-start | bytes 3076
  7.2 110.0 %all-gather.2.cloned.1.call-start = ((), (), s32[]{:S(2)}) async-start(), calls=%async_computation.2 | async-start | bytes 10616832 | tf_op jit(solution)/shard_map/all_gather | solution.py:94
  94.3 8.4 %collective-permute-start = (bf16[2,1,64,512]{3,2,1,0:T(8,128)(2,1)S(1)}, bf16[2,1,64,512]{3,2,1,0:T(8,128)(2,1)S(1)}, u32[]{:S(2)}, u32[]{:S(2)}) collective-permute-start(bf16[2,1,64,512]{3,2,1,0:T(8,128)(2,1)S(1)} %all_gather.14), channel_id=1, source_target_pairs={{0,2},{1,3},{4,6},{5,7},{8,10},{9,11},{12,14},{13,15},{16,18},{17,... | collective-permute-start | bytes 393224 | tf_op jit(solution)/shard_map/ppermute | solution.py:16
  102.8 8.1 %collective-permute-start.1 = (bf16[4,1,64,512]{3,2,1,0:T(8,128)(2,1)S(1)}, bf16[4,1,64,512]{3,2,1,0:T(8,128)(2,1)S(1)}, u32[]{:S(2)}, u32[]{:S(2)}) collective-permute-start(bf16[4,1,64,512]{3,2,1,0:T(8,128)(2,1)S(1)} %constant_dynamic-update-slice_fusion), channel_id=1, source_target_pairs={{0,4},{4,8},{8,12},{1,5},{5,9},{9,13},{2,6},{6,10},{10,14},{3,7},{... | collective-permute-start | bytes 786440 | tf_op jit(solution)/shard_map/ppermute | solution.py:27
  105.8 9.2 %collective-permute-start.2 = (bf16[4,1,64,512]{3,2,1,0:T(8,128)(2,1)S(1)}, bf16[4,1,64,512]{3,2,1,0:T(8,128)(2,1)S(1)}, u32[]{:S(2)}, u32[]{:S(2)}) collective-permute-start(bf16[4,1,64,512]{3,2,1,0:T(8,128)(2,1)S(1)} %constant_dynamic-update-slice_fusion), channel_id=1, source_target_pairs={{4,0},{8,4},{12,8},{5,1},{9,5},{13,9},{6,2},{10,6},{14,10},{7,3},{... | collective-permute-start | bytes 786440 | tf_op jit(solution)/shard_map/ppermute | solution.py:29
  117.2 14.5 %copy-start.1 = (bf16[3,3,3,512,256]{4,3,2,1,0:T(8,128)(2,1)S(1)}, bf16[3,3,3,512,256]{4,3,2,1,0:T(8,128)(2,1)}, u32[]{:S(2)}) copy-start(bf16[3,3,3,512,256]{4,3,2,1,0:T(8,128)(2,1)} %all-gather.2.cloned.1.call-done) | copy-start | bytes 21233668
  117.2 15.8 %copy-start.6 = (bf16[2,1,64,512]{3,2,1,0:T(8,128)(2,1)S(1)}, bf16[2,1,64,512]{3,2,1,0:T(8,128)(2,1)}, u32[]{:S(2)}) copy-start(bf16[2,1,64,512]{3,2,1,0:T(8,128)(2,1)} %get-tuple-element.38) | copy-start | bytes 393220
  117.2 16.8 %copy-start.5 = (bf16[2,1,64,512]{3,2,1,0:T(8,128)(2,1)S(1)}, bf16[2,1,64,512]{3,2,1,0:T(8,128)(2,1)}, u32[]{:S(2)}) copy-start(bf16[2,1,64,512]{3,2,1,0:T(8,128)(2,1)} %get-tuple-element.35) | copy-start | bytes 393220
  117.2 17.2 %copy-start.4 = (bf16[2,1,64,512]{3,2,1,0:T(8,128)(2,1)S(1)}, bf16[2,1,64,512]{3,2,1,0:T(8,128)(2,1)}, u32[]{:S(2)}) copy-start(bf16[2,1,64,512]{3,2,1,0:T(8,128)(2,1)} %get-tuple-element.37) | copy-start | bytes 393220
  123.6 11.8 %copy-start.3 = (bf16[2,1,64,512]{3,2,1,0:T(8,128)(2,1)S(1)}, bf16[2,1,64,512]{3,2,1,0:T(8,128)(2,1)}, u32[]{:S(2)}) copy-start(bf16[2,1,64,512]{3,2,1,0:T(8,128)(2,1)} %get-tuple-element.34) | copy-start | bytes 393220
Sparse Core Ops, SparseCore 0:
  9.6 92.6 all-gather.1
where the time goes:
time: 145 us; the launch traced here: 144 us
  blocking collectives  78.5 us (54%)
  matrix products  23.1 us (16%)
  between operations  14.5 us (10%)
  waiting for transfers between devices  12.9 us (9%)
  starting transfers between devices  8.43 us (6%)
  local copies, waits for them, and re-layouts  3.52 us (2%)
  other arithmetic  2.8 us (2%)
    psum x2, blocking collectives, normalize(): lax.psum((jnp.sum(grouped, axis=(0, 2)), jnp.sum(grouped * grouped, axis=...  40.8 us
    dot_general x27, matrix products, convolve(): jnp.dot(window, piece[time_tap, row_tap, col_tap], preferred_element_type...  18.8 us
    all_gather x1, blocking collectives, attend(): key_piece = lax.all_gather(keyed, 'space', axis=0, tiled=True)  14.3 us
    all_gather x1, blocking collectives, attend(): value_piece = lax.all_gather(valued, 'space', axis=0, tiled=True)  13.9 us
    ppermute x1, waiting for transfers between devices, shifted_2(): return lax.ppermute(x, axis, pairs)  4.29 us
    ppermute x1, waiting for transfers between devices, padded_2(): lax.ppermute(head, axis, [((i + 1) % count, i) for i in range(ends)])  4.13 us
    ppermute x1, starting transfers between devices, shifted_2(): return lax.ppermute(x, axis, pairs)  4.12 us
    ppermute x1, waiting for transfers between devices, padded_2(): lax.ppermute(tail, axis, [(i, (i + 1) % count) for i in range(ends)])  3.8 us
  transfers between devices with their start and end apart: 4, of which 3 were waited for; matrix products, arithmetic and copies ran while one was open for 7% of the time, Pallas kernels for 0%

commit v1 on v0

v1 whole, which is shorter than its diff:
```python
import functools

import jax
import jax.numpy as jnp
from jax import lax
from jax.experimental import pallas as pl
from jax.experimental.pallas import tpu as pltpu
from jax.sharding import PartitionSpec as P

D = 512
NGROUP = 32
EPSILON = 1e-06
LANES = 128
BLOCKS = D // LANES
GROUP = D // NGROUP
MESH = pl.DeviceIdType.MESH
F32 = jnp.float32
BF16 = jnp.bfloat16


def group_total(v):
    lane = lax.broadcasted_iota(jnp.int32, v.shape, 1)
    width = v.shape[1]
    step = 1
    while step < GROUP:
        above = pltpu.roll(v, width - step, 1)
        below = pltpu.roll(v, step, 1)
        v = v + jnp.where((lane // step) % 2 == 0, above, below)
        step *= 2
    return v


def packed_moments(values, first_block):
    sums = jnp.sum(values, axis=0, keepdims=True)
    squares = jnp.sum(values * values, axis=0, keepdims=True)
    rows = jnp.concatenate([sums, squares] * 4, axis=0)
    totals = group_total(rows)
    place = lax.broadcasted_iota(jnp.int32, (1, LANES), 1) % GROUP
    packed = jnp.zeros((1, LANES), F32)
    for block in range(values.shape[1] // LANES):
        piece = totals[:, block * LANES : (block + 1) * LANES]
        packed = jnp.where(place == first_block + block, piece[0:1], packed)
        packed = jnp.where(place == BLOCKS + first_block + block, piece[1:2], packed)
    return packed


def moments(packed, population):
    place = lax.broadcasted_iota(jnp.int32, (2 * BLOCKS, LANES), 1) % GROUP
    row = lax.broadcasted_iota(jnp.int32, (2 * BLOCKS, LANES), 0)
    wide = jnp.broadcast_to(packed, (2 * BLOCKS, LANES))
    spread_out = group_total(jnp.where(place == row, wide, 0.0)) / population
    mean = jnp.concatenate([spread_out[k : k + 1] for k in range(BLOCKS)], axis=1)
    square = jnp.concatenate([spread_out[BLOCKS + k : BLOCKS + k + 1] for k in range(BLOCKS)], axis=1)
    variance = jnp.maximum(square - mean * mean, 0.0)
    return mean, lax.rsqrt(variance + EPSILON)


def kernel(
    S, T, C, W,
    x, g1, g2, wq_hbm, wk_hbm, wv_hbm, wo_hbm, wc_hbm,
    att_out, conv_out,
    wq, wk, wv, wo, wc,
    stat1_src, stat1, stat2_src, stat2, gall1, gall2,
    xall, tokens, att_src, att_in, dsrc, dall, act, part_src, part,
    wsem, send_sem, gsem, s1sem, xsem, s2sem, asem, dsem, psend, psem,
):
    g = lax.axis_index("groups")
    h = lax.axis_index("space")
    t = lax.axis_index("tm")
    c = lax.axis_index("chan")
    n = S * T * C
    me = (h * T + t) * C + c
    half = D // C
    Kc = D // T
    NF = T * C
    other = lax.rem(c + 1, C)

    def place(i):
        return (g, i // (T * C), lax.rem(i // C, T), lax.rem(i, C))

    loads = [
        pltpu.make_async_copy(src, dst, wsem.at[i])
        for i, (src, dst) in enumerate(
            [(wk_hbm, wk), (wq_hbm, wq), (wv_hbm, wv), (wo_hbm, wo), (wc_hbm, wc)]
        )
    ]
    for load in loads:
        load.start()

    barrier = pltpu.get_barrier_semaphore()

    @pl.loop(1, n)
    def _(i):
        pl.semaphore_signal(barrier, inc=1, device_id=place(lax.rem(me + i, n)), device_id_type=MESH)

    own = x[...].reshape(C * W, half).astype(F32)
    stat1_src[...] = packed_moments(own, c * (half // LANES))
    gall1[c] = g1[...]
    gall2[c] = g2[...]
    stat1[me] = stat1_src[...]
    xall[h * C + c] = x[c, 0]
    pl.semaphore_wait(barrier, n - 1)

    def send_stat(src, dst, sends, recvs):
        @pl.loop(1, n)
        def _(i):
            pltpu.make_async_remote_copy(
                src_ref=src, dst_ref=dst.at[me], send_sem=sends, recv_sem=recvs,
                device_id=place(lax.rem(me + i, n)), device_id_type=MESH,
            ).start()

    def drain(ref, sem):
        pltpu.make_async_copy(ref, ref, sem).wait()

    send_stat(stat1_src, stat1, send_sem.at[0], s1sem)
    gains = [
        pltpu.make_async_remote_copy(
            src_ref=src, dst_ref=dst.at[c], send_sem=send_sem.at[1 + k], recv_sem=gsem.at[k],
            device_id=(g, h, t, other), device_id_type=MESH,
        )
        for k, (src, dst) in enumerate([(g1, gall1), (g2, gall2)])
    ]
    for copy in gains:
        copy.start()
    for dh in list(range(1, S)) + [0]:
        for dc in range(C):
            if dh == 0 and dc == 0:
                continue
            frame = lax.rem(c + dc, C)
            pltpu.make_async_remote_copy(
                src_ref=x.at[frame, 0], dst_ref=xall.at[h * C + c],
                send_sem=send_sem.at[3], recv_sem=xsem,
                device_id=(g, lax.rem(h + dh, S), t, frame), device_id_type=MESH,
            ).start()

    drain(stat1.at[pl.ds(0, n - 1)], s1sem)
    for copy in gains:
        copy.wait()
    population = float(n * W * GROUP)
    mean1, scale1 = moments(jnp.sum(stat1[...], axis=0), population)
    gain1 = jnp.concatenate([gall1[k] for k in range(C)], axis=1)
    gain2 = jnp.concatenate([gall2[k] for k in range(C)], axis=1)

    drain(xall.at[pl.ds(0, S * C - 1)], xsem)

    @pl.loop(0, S, unroll=S <= 4)
    def _(r):
        for k in range(C):
            lanes = slice(k * half, (k + 1) * half)
            value = xall[r * C + k].astype(F32)
            value = (value - mean1[:, lanes]) * scale1[:, lanes] * gain1[:, lanes]
            tokens[r, :, lanes] = value.astype(BF16)

    mine = tokens[h]
    every = tokens[...].reshape(S * W, D)
    loads[0].wait()
    keyed = jnp.dot(every, wk[...], preferred_element_type=F32).astype(BF16)
    loads[1].wait()
    queries = jnp.dot(mine, wq[...], preferred_element_type=F32).astype(BF16)
    scores = lax.dot_general(
        queries, keyed, (((1,), (1,)), ((), ())), preferred_element_type=F32
    ) * (D ** (-0.5))
    loads[2].wait()
    valued = jnp.dot(every, wv[...], preferred_element_type=F32).astype(BF16)
    weights = jnp.exp(scores - jnp.max(scores, axis=1, keepdims=True))
    mass = jnp.sum(weights, axis=1, keepdims=True)
    mixed = jnp.dot(weights.astype(BF16), valued, preferred_element_type=F32)
    mixed = (mixed / mass).astype(BF16)
    loads[3].wait()
    attended = jnp.dot(mixed, wo[...], preferred_element_type=F32).astype(BF16)

    source = jnp.concatenate([xall[h * C + k] for k in range(C)], axis=1).astype(F32)
    resid = (source - mean1) + attended.astype(F32)
    for k in range(T):
        dsrc[k] = resid[:, k * Kc : (k + 1) * Kc].astype(BF16)
    for k in range(C):
        att_src[k] = attended[:, k * half : (k + 1) * half]
    stat2_src[...] = packed_moments(resid, 0)
    stat2[me] = stat2_src[...]
    send_stat(stat2_src, stat2, send_sem.at[4], s2sem)

    frame_at = t * C + c

    def send_rows(dh, skip_self):
        for dt in range(T):
            for dc in range(C):
                if skip_self and dt == 0 and dc == 0:
                    continue
                to = lax.rem(t + dt, T)
                pltpu.make_async_remote_copy(
                    src_ref=dsrc.at[to], dst_ref=dall.at[1 - dh, frame_at],
                    send_sem=send_sem.at[6 + dh], recv_sem=dsem.at[1 - dh],
                    device_id=(g, h + dh, to, lax.rem(c + dc, C)), device_id_type=MESH,
                ).start()

    @pl.when(h > 0)
    def _():
        send_rows(-1, False)

    @pl.when(h < S - 1)
    def _():
        send_rows(1, False)

    send_rows(0, True)
    back = pltpu.make_async_remote_copy(
        src_ref=att_src.at[other], dst_ref=att_in, send_sem=send_sem.at[8], recv_sem=asem,
        device_id=(g, h, t, other), device_id_type=MESH,
    )
    back.start()
    dall[1, frame_at] = dsrc[t]
    att_out[c, 0] = att_src[c]
    act[0:2] = jnp.zeros((2,) + act.shape[1:], BF16)

    drain(stat2.at[pl.ds(0, n - 1)], s2sem)
    mean2, scale2 = moments(jnp.sum(stat2[...], axis=0), population)
    factor = scale2 * gain2

    def sliced(v):
        out = v[:, 0:Kc]
        for k in range(1, T):
            out = jnp.where(t == k, v[:, k * Kc : (k + 1) * Kc], out)
        return out

    mean_t = sliced(mean2)
    factor_t = sliced(factor)
    column = lax.broadcasted_iota(jnp.int32, (W, Kc), 0)

    def activate(row):
        @pl.loop(0, NF, unroll=NF <= 4)
        def _(f):
            v = (dall[row, f].astype(F32) - mean_t) * factor_t
            a = v / (1.0 + jnp.exp(-v))
            left = jnp.where(column == 0, 0.0, pltpu.roll(a, 1, 0))
            right = jnp.where(column == W - 1, 0.0, pltpu.roll(a, W - 1, 0))
            for e, piece in enumerate((left, a, right)):
                k = row * 3 + e
                act[f + 2, :, k * Kc : (k + 1) * Kc] = piece.astype(BF16)

    def blank(row):
        act[2:, :, row * 3 * Kc : (row + 1) * 3 * Kc] = jnp.zeros((NF, W, 3 * Kc), BF16)

    drain(dall.at[1, pl.ds(0, NF - 1)], dsem.at[1])
    activate(1)

    @pl.when(h > 0)
    def _():
        drain(dall.at[0], dsem.at[0])
        activate(0)

    @pl.when(h == 0)
    def _():
        blank(0)

    @pl.when(h < S - 1)
    def _():
        drain(dall.at[2], dsem.at[2])
        activate(2)

    @pl.when(h == S - 1)
    def _():
        blank(2)

    loads[4].wait()

    def partial(to):
        total = None
        for a in range(3):
            window = act[pl.ds(to * C + a, C)].reshape(C * W, 9 * Kc)
            product = jnp.dot(window, wc[a], preferred_element_type=F32)
            total = product if total is None else total + product
        return total

    returns = []
    for dt in range(1, T):
        to = lax.rem(t + dt, T)
        part_src[dt - 1] = partial(to)
        copy = pltpu.make_async_remote_copy(
            src_ref=part_src.at[dt - 1], dst_ref=part.at[dt - 1],
            send_sem=psend.at[dt - 1], recv_sem=psem.at[dt - 1],
            device_id=(g, h, to, c), device_id_type=MESH,
        )
        copy.start()
        returns.append(copy)
    total = partial(t)
    back.wait()
    att_out[other, 0] = att_in[...]

    drain(stat1.at[pl.ds(0, n - 1)], send_sem.at[0])
    drain(xall.at[pl.ds(0, S * C - 1)], send_sem.at[3])
    drain(stat2.at[pl.ds(0, n - 1)], send_sem.at[4])
    drain(dall.at[1, pl.ds(0, NF - 1)], send_sem.at[6])

    @pl.when(h > 0)
    def _():
        drain(dall.at[0], send_sem.at[5])

    @pl.when(h < S - 1)
    def _():
        drain(dall.at[2], send_sem.at[7])

    for k, copy in enumerate(returns):
        copy.wait()
        total = total + part[k]
    conv_out[...] = total.reshape(conv_out.shape).astype(BF16)


def on_device(S, T, C, x, g1, g2, wq, wk, wv, wo, wc):
    frames, rows, W, half = x.shape
    assert frames == C and rows == 1 and half * C == D
    Kc = wc.shape[3]
    assert Kc * T == D
    n, NF = S * T * C, T * C
    wc = wc.reshape(3, 9 * Kc, half)
    vmem = pl.BlockSpec(memory_space=pltpu.VMEM)
    hbm = pl.BlockSpec(memory_space=pl.ANY)
    out = jax.ShapeDtypeStruct(x.shape, BF16)
    dma = pltpu.SemaphoreType.DMA
    return pl.pallas_call(
        functools.partial(kernel, S, T, C, W),
        out_shape=(out, out),
        in_specs=[vmem] * 3 + [hbm] * 5,
        out_specs=(vmem, vmem),
        scratch_shapes=[
            *[pltpu.VMEM((D, D), BF16)] * 4,
            pltpu.VMEM(wc.shape, BF16),
            pltpu.VMEM((1, LANES), F32),
            pltpu.VMEM((n, 1, LANES), F32),
            pltpu.VMEM((1, LANES), F32),
            pltpu.VMEM((n, 1, LANES), F32),
            pltpu.VMEM((C, 1, half), F32),
            pltpu.VMEM((C, 1, half), F32),
            pltpu.VMEM((S * C, W, half), BF16),
            pltpu.VMEM((S, W, D), BF16),
            pltpu.VMEM((C, W, half), BF16),
            pltpu.VMEM((W, half), BF16),
            pltpu.VMEM((T, W, Kc), BF16),
            pltpu.VMEM((3, NF, W, Kc), BF16),
            pltpu.VMEM((NF + 2, W, 9 * Kc), BF16),
            pltpu.VMEM((max(T - 1, 1), C * W, half), F32),
            pltpu.VMEM((max(T - 1, 1), C * W, half), F32),
            dma((5,)),
            dma((9,)),
            dma((2,)),
            dma(()),
            dma(()),
            dma(()),
            dma(()),
            dma((3,)),
            dma((max(T - 1, 1),)),
            dma((max(T - 1, 1),)),
        ],
        compiler_params=pltpu.CompilerParams(collective_id=0, has_side_effects=True),
    )(x, g1.reshape(1, half), g2.reshape(1, half), wq, wk, wv, wo, wc)


def solution(mesh):
    S, T, C = mesh.shape["space"], mesh.shape["tm"], mesh.shape["chan"]
    placed = (
        P(("groups", "tm"), "space", None, "chan"),
        P("chan"),
        P("chan"),
        P(),
        P(),
        P(),
        P(),
        P(None, None, None, "tm", "chan"),
    )
    return jax.shard_map(
        functools.partial(on_device, S, T, C),
        mesh=mesh,
        in_specs=placed,
        out_specs=(
            P(("groups", "tm"), "space", None, "chan"),
            P(("groups", "tm"), "space", None, "chan"),
        ),
        check_vma=False,
    )
```

time: 145 us -> 31.5 us (0.22)
  blocking collectives: 78.5 us -> 0 us
  Pallas kernels: 0 us -> 27.6 us
  matrix products: 23.1 us -> 0 us
  between operations: 14.5 us -> 0.64 us
  waiting for transfers between devices: 12.9 us -> 0 us
  starting transfers between devices: 8.43 us -> 0 us
  other arithmetic: 2.8 us -> 0 us
    psum x2 -> x0, blocking collectives: 40.8 us -> none  [normalize(): lax.psum((jnp.sum(grouped, axis=(0, 2)), jnp.sum(grouped * grouped, axis=...]
    all_gather x3 -> x0, blocking collectives: 30.1 us -> none  [the longest x1 14.3 us: attend(): key_piece = lax.all_gather(keyed, 'space', axis=0, tiled=True)]
    pallas_call x0 -> x1, Pallas kernels: none -> 27.6 us  [on_device(): pl.pallas_call(functools.partial(kernel, S, T, C, W), out_shape=(out, out...]
    dot_general x31 -> x0, matrix products: 23.1 us -> none  [the longest x27 18.8 us: convolve(): jnp.dot(window, piece[time_tap, row_tap, col_tap], preferred_element_type...]
    ppermute x3 -> x0, waiting for transfers between devices: 12.2 us -> none  [the longest x1 4.29 us: shifted_2(): return lax.ppermute(x, axis, pairs)]
    ppermute x3 -> x0, starting transfers between devices: 8.39 us -> none  [the longest x1 4.12 us: shifted_2(): return lax.ppermute(x, axis, pairs)]
    all_to_all x2 -> x0, blocking collectives: 7.58 us -> none  [the longest x1 3.79 us: attend(): lax.all_to_all(tokens, 'chan', split_axis=0, concat_axis=1, tiled=True)]
    unnamed x18 -> x2, local copies, waits for them, and re-layouts: 0.68 us -> 2.95 us
  transfers between devices with their start and end apart: 4 -> 0, of which waited for: 3 -> 0; matrix products, arithmetic and copies ran while one was open for 7% -> 0% of each run, Pallas kernels for 0% -> 0%
where the time goes in v1:
time: 31.5 us; the launch traced here: 31.2 us
  Pallas kernels  27.6 us (88%)
  local copies, waits for them, and re-layouts  2.95 us (9%)
  between operations  0.64 us (2%)
    pallas_call x1, Pallas kernels, on_device(): pl.pallas_call(functools.partial(kernel, S, T, C, W), out_shape=(out, out...  27.6 us
    unnamed x2, local copies, waits for them, and re-layouts  2.95 us

profile of v1, /device:TPU:0, one launch (start us, length us, event | category | flops | bytes accessed | tf_op | source)
XLA Modules:
  0.0 31.2 jit_solution(374079749527019676)
XLA Ops:
  0.6 27.6 %shard_map.95 = (bf16[2,1,64,256]{3,2,1,0:T(8,128)(2,1)}, bf16[2,1,64,256]{3,2,1,0:T(8,128)(2,1)}) custom-call(bf16[2,1,64,256]{3,2,1,0:T(8,128)(2,1)} %x.1, f32[1,256]{1,0:T(1,128)} %bitcast.4, f32[1,256]{1,0:T(1,128)} %bitcast.5, bf16[512,512]{1,0:T(8,128)(2,1)} %wq_hbm.1, bf16[512,512]{1,0:T(8,128)(2,1)} %wk_hbm.1, bf16[512,512]{1,0:T(8,128)(2,1)} %wv_hbm.1, ...), custom_call_target="tpu_custom_call" | custom-call | tf_op jit(solution)/shard_map/pallas_call | solution.py:318
  28.3 1.5 %copy.12 = bf16[2,1,64,256]{3,2,1,0:T(8,128)(2,1)} copy(bf16[2,1,64,256]{3,2,1,0:T(8,128)(2,1)} %get-tuple-element.4) | data formatting | bytes 131072
  29.8 1.5 %copy.13 = bf16[2,1,64,256]{3,2,1,0:T(8,128)(2,1)} copy(bf16[2,1,64,256]{3,2,1,0:T(8,128)(2,1)} %get-tuple-element.5) | data formatting | bytes 131072

commit v2 on v1

--- a/solution.py
+++ b/solution.py
@@ -57,12 +57,12 @@
 
 def kernel(
     S, T, C, W,
-    x, g1, g2, wq_hbm, wk_hbm, wv_hbm, wo_hbm, wc_hbm,
+    x_hbm, g1, g2, wq_hbm, wk_hbm, wv_hbm, wo_hbm, wc_hbm,
     att_out, conv_out,
-    wq, wk, wv, wo, wc,
+    x, wq, wk, wv, wo, wc,
     stat1_src, stat1, stat2_src, stat2, gall1, gall2,
     xall, tokens, att_src, att_in, dsrc, dall, act, part_src, part,
-    wsem, send_sem, gsem, s1sem, xsem, s2sem, asem, dsem, psend, psem,
+    xload, wsem, send_sem, gsem, s1sem, xsem, s2sem, asem, dsem, psend, psem,
 ):
     g = lax.axis_index("groups")
     h = lax.axis_index("space")
@@ -78,6 +78,18 @@
     def place(i):
         return (g, i // (T * C), lax.rem(i // C, T), lax.rem(i, C))
 
+    first = [
+        pltpu.make_async_copy(src, dst, xload.at[i])
+        for i, (src, dst) in enumerate([(x_hbm, x), (g1, gall1.at[c]), (g2, gall2.at[c])])
+    ]
+    for load in first:
+        load.start()
+    barrier = pltpu.get_barrier_semaphore()
+
+    @pl.loop(1, n)
+    def _(i):
+        pl.semaphore_signal(barrier, inc=1, device_id=place(lax.rem(me + i, n)), device_id_type=MESH)
+
     loads = [
         pltpu.make_async_copy(src, dst, wsem.at[i])
         for i, (src, dst) in enumerate(
@@ -87,16 +99,10 @@
     for load in loads:
         load.start()
 
-    barrier = pltpu.get_barrier_semaphore()
-
-    @pl.loop(1, n)
-    def _(i):
-        pl.semaphore_signal(barrier, inc=1, device_id=place(lax.rem(me + i, n)), device_id_type=MESH)
-
+    for load in first:
+        load.wait()
     own = x[...].reshape(C * W, half).astype(F32)
     stat1_src[...] = packed_moments(own, c * (half // LANES))
-    gall1[c] = g1[...]
-    gall2[c] = g2[...]
     stat1[me] = stat1_src[...]
     xall[h * C + c] = x[c, 0]
     pl.semaphore_wait(barrier, n - 1)
@@ -273,7 +279,7 @@
     returns = []
     for dt in range(1, T):
         to = lax.rem(t + dt, T)
-        part_src[dt - 1] = partial(to)
+        part_src[dt - 1] = partial(to).astype(BF16)
         copy = pltpu.make_async_remote_copy(
             src_ref=part_src.at[dt - 1], dst_ref=part.at[dt - 1],
             send_sem=psend.at[dt - 1], recv_sem=psem.at[dt - 1],
@@ -300,8 +306,13 @@
 
     for k, copy in enumerate(returns):
         copy.wait()
-        total = total + part[k]
+        total = total + part[k].astype(F32)
     conv_out[...] = total.reshape(conv_out.shape).astype(BF16)
+
+
+def hand_over(att_in, conv_in, att_out, conv_out):
+    att_out[...] = att_in[...]
+    conv_out[...] = conv_in[...]
 
 
 def on_device(S, T, C, x, g1, g2, wq, wk, wv, wo, wc):
@@ -315,12 +326,14 @@
     hbm = pl.BlockSpec(memory_space=pl.ANY)
     out = jax.ShapeDtypeStruct(x.shape, BF16)
     dma = pltpu.SemaphoreType.DMA
-    return pl.pallas_call(
+    kept = pltpu.VMEM(x.shape, BF16)
+    results = pl.pallas_call(
         functools.partial(kernel, S, T, C, W),
-        out_shape=(out, out),
-        in_specs=[vmem] * 3 + [hbm] * 5,
+        out_shape=(kept, kept),
+        in_specs=[hbm] * 8,
         out_specs=(vmem, vmem),
         scratch_shapes=[
+            pltpu.VMEM(x.shape, BF16),
             *[pltpu.VMEM((D, D), BF16)] * 4,
             pltpu.VMEM(wc.shape, BF16),
             pltpu.VMEM((1, LANES), F32),
@@ -336,8 +349,9 @@
             pltpu.VMEM((T, W, Kc), BF16),
             pltpu.VMEM((3, NF, W, Kc), BF16),
             pltpu.VMEM((NF + 2, W, 9 * Kc), BF16),
-            pltpu.VMEM((max(T - 1, 1), C * W, half), F32),
-            pltpu.VMEM((max(T - 1, 1), C * W, half), F32),
+            pltpu.VMEM((max(T - 1, 1), C * W, half), BF16),
+            pltpu.VMEM((max(T - 1, 1), C * W, half), BF16),
+            dma((3,)),
             dma((5,)),
             dma((9,)),
             dma((2,)),
@@ -351,6 +365,9 @@
         ],
         compiler_params=pltpu.CompilerParams(collective_id=0, has_side_effects=True),
     )(x, g1.reshape(1, half), g2.reshape(1, half), wq, wk, wv, wo, wc)
+    return pl.pallas_call(
+        hand_over, out_shape=(out, out), in_specs=[vmem] * 2, out_specs=(vmem, vmem),
+    )(*[pltpu.with_memory_space_constraint(r, pltpu.VMEM) for r in results])
 
 
 def solution(mesh):

time: 31.5 us -> 26.6 us (0.84)
  local copies, waits for them, and re-layouts: 2.95 us -> 0 us
  Pallas kernels: 27.6 us -> 25.8 us
    unnamed x2 -> x0, local copies, waits for them, and re-layouts: 2.95 us -> none
    pallas_call x1 -> x2, Pallas kernels: 27.6 us -> 25.8 us  [the longest x1 25.1 us: on_device(): pl.pallas_call(functools.partial(kernel, S, T, C, W), out_shape=(kept, ke...]
where the time goes in v2:
time: 26.6 us; the launch traced here: 26.4 us
  Pallas kernels  25.8 us (97%)
  between operations  0.64 us (2%)
    pallas_call x1, Pallas kernels, on_device(): pl.pallas_call(functools.partial(kernel, S, T, C, W), out_shape=(kept, ke...  25.1 us
    pallas_call x1, Pallas kernels, on_device(): pl.pallas_call(hand_over, out_shape=(out, out), in_specs=[vmem] * 2, out_...  0.66 us

profile of v2, /device:TPU:0, one launch (start us, length us, event | category | flops | bytes accessed | tf_op | source)
XLA Modules:
  0.0 26.4 jit_solution(7352940706675465165)
XLA Ops:
  0.6 25.1 %shard_map.95 = (bf16[2,1,64,256]{3,2,1,0:T(8,128)(2,1)S(1)}, bf16[2,1,64,256]{3,2,1,0:T(8,128)(2,1)S(1)}) custom-call(bf16[2,1,64,256]{3,2,1,0:T(8,128)(2,1)} %x_hbm.1, f32[1,256]{1,0:T(1,128)} %bitcast.4, f32[1,256]{1,0:T(1,128)} %bitcast.5, bf16[512,512]{1,0:T(8,128)(2,1)} %wq_hbm.1, bf16[512,512]{1,0:T(8,128)(2,1)} %wk_hbm.1, bf16[512,512]{1,0:T(8,128)(2,1)} %wv_hbm.1, ...), custom_call_target="tpu_custom_call" | custom-call | tf_op jit(solution)/shard_map/pallas_call | solution.py:330
  25.8 0.7 %shard_map.96 = (bf16[2,1,64,256]{3,2,1,0:T(8,128)(2,1)}, bf16[2,1,64,256]{3,2,1,0:T(8,128)(2,1)}) custom-call(bf16[2,1,64,256]{3,2,1,0:T(8,128)(2,1)S(1)} %get-tuple-element.4.att_in, bf16[2,1,64,256]{3,2,1,0:T(8,128)(2,1)S(1)} %get-tuple-element.5.conv_in), custom_call_target="tpu_custom_call" | custom-call | tf_op jit(solution)/shard_map/pallas_call | solution.py:368

commit v3 on v2

--- a/solution.py
+++ b/solution.py
@@ -14,6 +14,7 @@
 BLOCKS = D // LANES
 GROUP = D // NGROUP
 MESH = pl.DeviceIdType.MESH
+REACH = 2
 F32 = jnp.float32
 BF16 = jnp.bfloat16
 
@@ -61,8 +62,8 @@
     att_out, conv_out,
     x, wq, wk, wv, wo, wc,
     stat1_src, stat1, stat2_src, stat2, gall1, gall2,
-    xall, tokens, att_src, att_in, dsrc, dall, act, part_src, part,
-    xload, wsem, send_sem, gsem, s1sem, xsem, s2sem, asem, dsem, psend, psem,
+    xall, tokens, keyed, valued, att_src, att_in, dsrc, dall, act, part_src, part,
+    xload, wsem, send_sem, upsem, downsem, onsem, gsem, s1sem, xsem, s2sem, asem, dsem, psend, psem,
 ):
     g = lax.axis_index("groups")
     h = lax.axis_index("space")
@@ -75,8 +76,18 @@
     NF = T * C
     other = lax.rem(c + 1, C)
 
-    def place(i):
-        return (g, i // (T * C), lax.rem(i // C, T), lax.rem(i, C))
+    def to_everyone(act_on):
+        def tile(dh):
+            row = lax.rem(h + dh, S)
+            for dt in range(T):
+                for dc in range(C):
+                    act_on((g, row, lax.rem(t + dt, T), lax.rem(c + dc, C)))
+
+        pl.loop(1, S, unroll=S <= 4)(tile)
+        for dt in range(T):
+            for dc in range(C):
+                if dt or dc:
+                    act_on((g, h, lax.rem(t + dt, T), lax.rem(c + dc, C)))
 
     first = [
         pltpu.make_async_copy(src, dst, xload.at[i])
@@ -86,9 +97,9 @@
         load.start()
     barrier = pltpu.get_barrier_semaphore()
 
-    @pl.loop(1, n)
-    def _(i):
-        pl.semaphore_signal(barrier, inc=1, device_id=place(lax.rem(me + i, n)), device_id_type=MESH)
+    to_everyone(
+        lambda where: pl.semaphore_signal(barrier, inc=1, device_id=where, device_id_type=MESH)
+    )
 
     loads = [
         pltpu.make_async_copy(src, dst, wsem.at[i])
@@ -108,12 +119,12 @@
     pl.semaphore_wait(barrier, n - 1)
 
     def send_stat(src, dst, sends, recvs):
-        @pl.loop(1, n)
-        def _(i):
-            pltpu.make_async_remote_copy(
+        to_everyone(
+            lambda where: pltpu.make_async_remote_copy(
                 src_ref=src, dst_ref=dst.at[me], send_sem=sends, recv_sem=recvs,
-                device_id=place(lax.rem(me + i, n)), device_id_type=MESH,
+                device_id=where, device_id_type=MESH,
             ).start()
+        )
 
     def drain(ref, sem):
         pltpu.make_async_copy(ref, ref, sem).wait()
@@ -128,16 +139,48 @@
     ]
     for copy in gains:
         copy.start()
-    for dh in list(range(1, S)) + [0]:
-        for dc in range(C):
-            if dh == 0 and dc == 0:
-                continue
-            frame = lax.rem(c + dc, C)
-            pltpu.make_async_remote_copy(
-                src_ref=x.at[frame, 0], dst_ref=xall.at[h * C + c],
-                send_sem=send_sem.at[3], recv_sem=xsem,
-                device_id=(g, lax.rem(h + dh, S), t, frame), device_id_type=MESH,
-            ).start()
+    def send_x(dh, dc, sem):
+        frame = lax.rem(c + dc, C)
+        pltpu.make_async_remote_copy(
+            src_ref=x.at[frame, 0], dst_ref=xall.at[h * C + c], send_sem=sem, recv_sem=xsem.at[h],
+            device_id=(g, h + dh, t, frame), device_id_type=MESH,
+        ).start()
+
+    reach = min(REACH, S - 1)
+    for dc in range(1, C):
+        send_x(0, dc, send_sem.at[3])
+    for d in range(reach, 0, -1):
+
+        @pl.when(h + d < S)
+        def _():
+            for dc in range(C):
+                send_x(d, dc, upsem.at[d - 1])
+
+        @pl.when(h >= d)
+        def _():
+            for dc in range(C):
+                send_x(-d, dc, downsem.at[d - 1])
+
+    def slots(r):
+        return xall.at[pl.ds(r * C, C)]
+
+    def hand_on(r, to, sem):
+        return pltpu.make_async_remote_copy(
+            src_ref=slots(r), dst_ref=slots(r), send_sem=sem, recv_sem=xsem.at[r],
+            device_id=(g, to, t, c), device_id_type=MESH,
+        )
+
+    for d in range(reach, S - 1):
+
+        @pl.when((h >= d) & (h < S - 1))
+        def _():
+            drain(slots(h - d), xsem.at[h - d])
+            hand_on(h - d, h + 1, onsem.at[0, d]).start()
+
+        @pl.when((h + d < S) & (h > 0))
+        def _():
+            drain(slots(h + d), xsem.at[h + d])
+            hand_on(h + d, h - 1, onsem.at[1, d]).start()
 
     drain(stat1.at[pl.ds(0, n - 1)], s1sem)
     for copy in gains:
@@ -147,30 +190,49 @@
     gain1 = jnp.concatenate([gall1[k] for k in range(C)], axis=1)
     gain2 = jnp.concatenate([gall2[k] for k in range(C)], axis=1)
 
-    drain(xall.at[pl.ds(0, S * C - 1)], xsem)
-
-    @pl.loop(0, S, unroll=S <= 4)
-    def _(r):
+    def row_tokens(r):
+        pieces = []
         for k in range(C):
             lanes = slice(k * half, (k + 1) * half)
             value = xall[r * C + k].astype(F32)
             value = (value - mean1[:, lanes]) * scale1[:, lanes] * gain1[:, lanes]
-            tokens[r, :, lanes] = value.astype(BF16)
-
-    mine = tokens[h]
-    every = tokens[...].reshape(S * W, D)
+            pieces.append(value.astype(BF16))
+        return jnp.concatenate(pieces, axis=1)
+
+    def project(first, stop):
+        rows = tokens[first:stop].reshape((stop - first) * W, D)
+        shape = (stop - first, W, D)
+        keyed[first:stop] = jnp.dot(rows, wk[...], preferred_element_type=F32).astype(BF16).reshape(shape)
+        valued[first:stop] = jnp.dot(rows, wv[...], preferred_element_type=F32).astype(BF16).reshape(shape)
+
+    drain(xall.at[pl.ds(0, C - 1)], xsem.at[h])
+    mine = row_tokens(h)
     loads[0].wait()
-    keyed = jnp.dot(every, wk[...], preferred_element_type=F32).astype(BF16)
     loads[1].wait()
+    loads[2].wait()
     queries = jnp.dot(mine, wq[...], preferred_element_type=F32).astype(BF16)
+    tokens[0] = mine
+
+    mirror = (2 * h) // S
+    place_h = h + mirror * (S - 1 - 2 * h)
+    for k in range(S - 1):
+        r = k + (k - place_h + S) // S
+        r = r + mirror * (S - 1 - 2 * r)
+
+        @pl.when(jnp.logical_not(((r + reach <= h) & (h < S - 1)) | ((r >= h + reach) & (h > 0))))
+        def _():
+            drain(slots(r), xsem.at[r])
+
+        tokens[k + 1] = row_tokens(r)
+
+    project(0, S)
+
     scores = lax.dot_general(
-        queries, keyed, (((1,), (1,)), ((), ())), preferred_element_type=F32
+        queries, keyed[...].reshape(S * W, D), (((1,), (1,)), ((), ())), preferred_element_type=F32
     ) * (D ** (-0.5))
-    loads[2].wait()
-    valued = jnp.dot(every, wv[...], preferred_element_type=F32).astype(BF16)
     weights = jnp.exp(scores - jnp.max(scores, axis=1, keepdims=True))
     mass = jnp.sum(weights, axis=1, keepdims=True)
-    mixed = jnp.dot(weights.astype(BF16), valued, preferred_element_type=F32)
+    mixed = jnp.dot(weights.astype(BF16), valued[...].reshape(S * W, D), preferred_element_type=F32)
     mixed = (mixed / mass).astype(BF16)
     loads[3].wait()
     attended = jnp.dot(mixed, wo[...], preferred_element_type=F32).astype(BF16)
@@ -292,7 +354,27 @@
     att_out[other, 0] = att_in[...]
 
     drain(stat1.at[pl.ds(0, n - 1)], send_sem.at[0])
-    drain(xall.at[pl.ds(0, S * C - 1)], send_sem.at[3])
+    drain(xall.at[pl.ds(0, C - 1)], send_sem.at[3])
+    for d in range(1, reach + 1):
+
+        @pl.when(h + d < S)
+        def _():
+            drain(slots(0), upsem.at[d - 1])
+
+        @pl.when(h >= d)
+        def _():
+            drain(slots(0), downsem.at[d - 1])
+
+    for d in range(reach, S - 1):
+
+        @pl.when((h >= d) & (h < S - 1))
+        def _():
+            drain(slots(0), onsem.at[0, d])
+
+        @pl.when((h + d < S) & (h > 0))
+        def _():
+            drain(slots(0), onsem.at[1, d])
+
     drain(stat2.at[pl.ds(0, n - 1)], send_sem.at[4])
     drain(dall.at[1, pl.ds(0, NF - 1)], send_sem.at[6])
 
@@ -343,7 +425,7 @@
             pltpu.VMEM((C, 1, half), F32),
             pltpu.VMEM((C, 1, half), F32),
             pltpu.VMEM((S * C, W, half), BF16),
-            pltpu.VMEM((S, W, D), BF16),
+            *[pltpu.VMEM((S, W, D), BF16)] * 3,
             pltpu.VMEM((C, W, half), BF16),
             pltpu.VMEM((W, half), BF16),
             pltpu.VMEM((T, W, Kc), BF16),
@@ -354,9 +436,12 @@
             dma((3,)),
             dma((5,)),
             dma((9,)),
+            dma((REACH,)),
+            dma((REACH,)),
+            dma((2, S)),
             dma((2,)),
             dma(()),
-            dma(()),
+            dma((S,)),
             dma(()),
             dma(()),
             dma((3,)),

time: 26.6 us -> 25.7 us (0.966)
  Pallas kernels: 25.8 us -> 24.9 us
    pallas_call x1, Pallas kernels: 25.1 us -> 24.3 us  [on_device(): pl.pallas_call(functools.partial(kernel, S, T, C, W), out_shape=(kept, ke...]
where the time goes in v3:
time: 25.7 us; the launch traced here: 25.6 us
  Pallas kernels  24.9 us (97%)
  between operations  0.64 us (2%)
    pallas_call x1, Pallas kernels, on_device(): pl.pallas_call(functools.partial(kernel, S, T, C, W), out_shape=(kept, ke...  24.3 us
    pallas_call x1, Pallas kernels, on_device(): pl.pallas_call(hand_over, out_shape=(out, out), in_specs=[vmem] * 2, out_...  0.66 us

profile of v3, /device:TPU:0, one launch (start us, length us, event | category | flops | bytes accessed | tf_op | source)
XLA Modules:
  0.0 25.6 jit_solution(13912787472694371595)
XLA Ops:
  0.6 24.3 %shard_map.95 = (bf16[2,1,64,256]{3,2,1,0:T(8,128)(2,1)S(1)}, bf16[2,1,64,256]{3,2,1,0:T(8,128)(2,1)S(1)}) custom-call(bf16[2,1,64,256]{3,2,1,0:T(8,128)(2,1)} %x_hbm.1, f32[1,256]{1,0:T(1,128)} %bitcast.4, f32[1,256]{1,0:T(1,128)} %bitcast.5, bf16[512,512]{1,0:T(8,128)(2,1)} %wq_hbm.1, bf16[512,512]{1,0:T(8,128)(2,1)} %wk_hbm.1, bf16[512,512]{1,0:T(8,128)(2,1)} %wv_hbm.1, ...), custom_call_target="tpu_custom_call" | custom-call | tf_op jit(solution)/shard_map/pallas_call | solution.py:412
  24.9 0.7 %shard_map.96 = (bf16[2,1,64,256]{3,2,1,0:T(8,128)(2,1)}, bf16[2,1,64,256]{3,2,1,0:T(8,128)(2,1)}) custom-call(bf16[2,1,64,256]{3,2,1,0:T(8,128)(2,1)S(1)} %get-tuple-element.4.att_in, bf16[2,1,64,256]{3,2,1,0:T(8,128)(2,1)S(1)} %get-tuple-element.5.conv_in), custom_call_target="tpu_custom_call" | custom-call | tf_op jit(solution)/shard_map/pallas_call | solution.py:453
